TPU v7x, 128 devices: a whole 4x4x4 slice. The times are simulated.
128 devices in a mesh: state: 32 (over x, y, core), mem: 4 (over z).
Axes of the slice: x: 4, y: 4, z: 4, core: 2. Of those that a mesh axis runs over, the one named last changes fastest.
Arguments:
- ensemble: bfloat16 [80, 1048576], P('mem', 'state'), may hold values from -6 to 6
- weights: bfloat16 [8192, 12, 128], P('state'), may hold values from 0 to 0.14941406
- seg_obs: int32 [8192, 12], P('state'), may hold values from 0 to 65535, as said below
- observed: float32 [65536], replicated, may hold values from -180 to 180
- inv_var: float32 [65536], replicated, may hold values from 0.0001 to 0.001
Outputs:
- analysis: bfloat16 [80, 1048576], P('mem', 'state')
Inputs may be any that keep to these rules, and one draw needn't show every extreme that they name: seg_obs names the observation that a slot's arc segment contributes to. Of the 3072 slots of the tiles of one index of state, exactly 96 name observations in each aligned block of 2048 observations; an observation may have any number of slots, or none.
All inputs are finite; a program needn't handle non-finite values.
Results may differ from a plain program's by a relative error of at most 0.0051.
Values may be sent and summed in bfloat16 or wider, within the bound.
A program may use at most 128 MiB of HBM per device.

v0:
```python
import math
import jax
import jax.numpy as jnp
from jax import lax
from jax.sharding import PartitionSpec as P

ITERS = 14


def sent_together(arrays, axis, split_dim, concat_dim, along):
    widths = [math.prod(a.shape[along:]) for a in arrays]
    both = jnp.concatenate(
        [a.reshape(*a.shape[:along], w) for a, w in zip(arrays, widths)], axis=along
    )
    out = lax.all_to_all(both, axis, split_axis=split_dim, concat_axis=concat_dim, tiled=True)
    parts = jnp.split(out, [sum(widths[:k]) for k in range(1, len(widths))], axis=along)
    return tuple((b.reshape(*out.shape[:along], *a.shape[along:]) for a, b in zip(arrays, parts)))


def copy_for_each(x, axis):
    peers = lax.axis_size(axis)
    return lax.all_to_all(jnp.broadcast_to(x[None], (peers, *x.shape)), axis, 0, 0, tiled=True)


def taken_together(x, axis):
    everything = copy_for_each(x, axis)
    return jnp.sum(everything, axis=0)


def in_one(arrays, axis):
    ends = [0]
    for a in arrays:
        ends.append(ends[-1] + a.size)
    subtotal = taken_together(jnp.concatenate([a.ravel() for a in arrays]), axis)
    return tuple((subtotal[b:e].reshape(a.shape) for a, b, e in zip(arrays, ends, ends[1:])))


def transform(gram, pull, members):
    identity = jnp.eye(members, dtype=jnp.float32)
    system = (members - 1.0) * identity + gram
    scaling = jnp.sqrt(jnp.sum(system * system))
    ynow = system / scaling
    znow = identity
    for step in range(ITERS):
        correct = 1.5 * identity - 0.5 * jnp.dot(znow, ynow, precision=lax.Precision.HIGHEST)
        ynow = jnp.dot(ynow, correct, precision=lax.Precision.HIGHEST)
        znow = jnp.dot(correct, znow, precision=lax.Precision.HIGHEST)
    root = znow / jnp.sqrt(scaling)
    shift = jnp.dot(
        root, jnp.dot(root, pull, precision=lax.Precision.HIGHEST), precision=lax.Precision.HIGHEST
    )
    mixed = shift[:, None] + math.sqrt(members - 1.0) * root
    mixed = mixed + (1.0 - jnp.sum(mixed, axis=0, keepdims=True)) / members
    return mixed.astype(jnp.bfloat16)


def statistics(everyone, obs_here, var_here, members):
    mean_obs = jnp.sum(everyone, axis=0) / members
    anomaly = everyone - mean_obs
    weighted = anomaly * var_here
    gram = jnp.dot(weighted, anomaly.T, precision=lax.Precision.HIGHEST)
    pull = jnp.dot(weighted, obs_here - mean_obs, precision=lax.Precision.HIGHEST)
    return (gram, pull)


def gather_members(shares):
    return lax.all_gather(shares.astype(jnp.bfloat16), "mem", axis=0, tiled=True).astype(
        jnp.float32
    )


def per_device(ensemble, weights, seg_obs, observed, inv_var):
    own_members, own_cells = ensemble.shape
    own_tiles, own_slots, tile_width = weights.shape
    obs_count = observed.shape[0]
    all_members = own_members * lax.axis_size("mem")
    blocks = ensemble.reshape(own_members, own_tiles, tile_width)
    values = jnp.einsum("ktc,tjc->tjk", blocks, weights, preferred_element_type=jnp.float32)
    values = values.reshape(own_tiles * own_slots, own_members)
    slot_ids = seg_obs.reshape(-1)
    share_width = obs_count // lax.axis_size("state")
    owner = slot_ids // share_width
    order = jnp.argsort(owner, stable=True)
    sorted_values = values[order]
    local_place = (slot_ids[order] % share_width).astype(jnp.float32)
    arrived, arrived_place = sent_together((sorted_values, local_place), "state", 0, 0, 1)
    landed = jax.ops.segment_sum(arrived, arrived_place.astype(jnp.int32), num_segments=share_width)
    shares = landed.T
    begin_at = lax.axis_index("state") * share_width
    obs_here = lax.dynamic_slice_in_dim(observed, begin_at, share_width)
    var_here = lax.dynamic_slice_in_dim(inv_var, begin_at, share_width)
    everyone = gather_members(shares)
    gram, pull = statistics(everyone, obs_here, var_here, all_members)
    gram, pull = in_one((gram, pull), "state")
    mixing = transform(gram, pull, all_members)
    regrouped = lax.all_to_all(ensemble, "mem", split_axis=1, concat_axis=0, tiled=True)
    updated = jnp.einsum("jk,js->ks", mixing, regrouped, preferred_element_type=jnp.float32).astype(
        jnp.bfloat16
    )
    return lax.all_to_all(updated, "mem", split_axis=0, concat_axis=1, tiled=True)


def solution(mesh):
    return jax.shard_map(
        per_device,
        mesh=mesh,
        in_specs=(P("mem", "state"), P("state", None, None), P("state", None), P(), P()),
        out_specs=P("mem", "state"),
        check_vma=False,
    )
```

profile of v0, /device:TPU:1, one launch (start us, length us, event | category | flops | bytes accessed | tf_op | source)
XLA Modules:
  0.0 159.3 jit_solution(11215360231634751820)
XLA Ops:
  0.0 0.8 copy.66
  1.0 5.8 %sort.17 = (s32[3072]{0:T(1024)}, s32[3072]{0:T(1024)S(1)}) sort(s32[3072]{0:T(1024)S(1)} %add_select_fusion.1, s32[3072]{0:T(1024)S(1)} %iota.88), dimensions={0}, to_apply=%region_0.1 | sort | flops 36864 | bytes 49152 | tf_op jit(solution)/shard_map/jit(argsort)/sort | solution.py:83
  6.7 17.4 %gather_fusion.1 = s32[3072]{0:T(1024)S(1)} fusion(s32[3072]{0:T(1024)S(1)} %reshape.116, s32[3072]{0:T(1024)S(1)} %fusion.37), kind=kCustom, calls=%fused_computation.1 | custom fusion | bytes 36864 | tf_op jit(solution)/shard_map/gather | solution.py:85
  24.3 0.3 copy.80
  24.7 1.0 copy-done.2
  25.7 2.7 %fusion = f32[256,12,20]{2,1,0:T(8,128)} fusion(bf16[20,256,128]{2,1,0:T(8,128)(2,1)S(1)} %slice.22, bf16[256,12,128]{2,0,1:T(8,128)(2,1)S(1)} %copy-done.2), kind=kOutput, calls=%fused_computation.4 | convolution fusion | flops 15728640 | bytes 2342912 | tf_op jit(solution)/shard_map/ktc,tjc->tjk/dot_general | solution.py:78
  28.4 1.6 %reshape.154 = f32[3072,20]{1,0:T(8,128)S(1)} reshape(f32[256,12,20]{2,1,0:T(8,128)} %fusion) | data formatting | bytes 491520 | tf_op jit(solution)/shard_map/reshape | solution.py:79
  30.0 8.1 %gather_fusion = f32[3072,20]{1,0:T(8,128)S(1)} fusion(f32[3072,20]{1,0:T(8,128)S(1)} %reshape.154, s32[3072]{0:T(1024)S(1)} %fusion.37), kind=kCustom, calls=%fused_computation | custom fusion | bytes 503808 | tf_op jit(solution)/shard_map/gather | solution.py:84
  38.2 0.5 copy.68
  38.7 0.8 pad_maximum_fusion
  39.5 8.6 %all-to-all-start = ((f32[32,96,21]{1,2,0:T(8,128)}), f32[32,96,21]{1,2,0:T(8,128)S(1)}, u32[]{:S(2)}, u32[]{:S(2)}) async-start(f32[32,96,21]{1,2,0:T(8,128)} %pad_maximum_fusion), calls=%async_computation | async-start | bytes 786432 | tf_op jit(solution)/shard_map/all_to_all | solution.py:15
  48.1 2.1 %all_to_all.41 = bf16[20,4,8192]{2,1,0:T(4,128)(2,1)S(1)} reshape(bf16[20,32768]{1,0:T(8,128)(2,1)S(1)} %copy-done.1) | data formatting | bytes 2621440 | tf_op jit(solution)/shard_map/all_to_all | solution.py:96
  50.2 1.9 %copy.74 = bf16[20,4,8192]{2,0,1:T(8,128)(2,1)} copy(bf16[20,4,8192]{2,1,0:T(4,128)(2,1)S(1)} %all_to_all.41) | data formatting | bytes 2621440 | tf_op jit(solution)/shard_map/all_to_all | solution.py:96
  52.1 0.7 dynamic_slice.6
  52.8 5.6 %all-to-all-done = f32[32,96,21]{1,2,0:T(8,128)S(1)} async-done(((f32[32,96,21]{1,2,0:T(8,128)}), f32[32,96,21]{1,2,0:T(8,128)S(1)}, u32[]{:S(2)}, u32[]{:S(2)}) %all-to-all-start) | async-done | bytes 258080 | tf_op jit(solution)/shard_map/all_to_all | solution.py:15
  58.3 5.0 %all-to-all-start.2 = ((bf16[20,4,8192]{2,0,1:T(8,128)(2,1)}), bf16[20,4,8192]{2,0,1:T(8,128)(2,1)S(1)}, u32[]{:S(2)}, u32[]{:S(2)}) async-start(bf16[20,4,8192]{2,0,1:T(8,128)(2,1)} %copy.74), calls=%async_computation.2 | async-start | bytes 3145728 | tf_op jit(solution)/shard_map/all_to_all | solution.py:96
  63.4 0.2 all_to_all.39
  63.7 1.7 %copy.71 = f32[3072,20]{1,0:T(8,128)} copy(f32[3072,20]{0,1:T(8,128)S(1)} %bitcast.118) | data formatting | bytes 491520 | tf_op jit(solution)/shard_map/split | solution.py:16
  65.3 17.5 %scatter_custom_fusion = f32[2048,20]{1,0:T(8,128)S(1)} fusion(s32[3072]{0:T(1024)S(1)} %bitcast.121, f32[3072,20]{1,0:T(8,128)} %copy.71, f32[]{:T(128)} %constant.44.clone.1), kind=kCustom, calls=%fused_computation.45 | custom fusion | flops 61440 | bytes 164352 | tf_op jit(solution)/shard_map/scatter-add | solution.py:87
  82.9 0.2 copy.72
  83.1 10.9 %all-gather = bf16[4,20,2048]{2,1,0:T(8,128)(2,1)S(1)} all-gather(bf16[1,20,2048]{2,1,0:T(8,128)(2,1)S(1)} %copy.72), channel_id=1, replica_groups=mesh['state'=32,'mem'=4] {'mem'}, dimensions={0}, use_global_device_ids=true | all-gather | bytes 409600 | tf_op jit(solution)/shard_map/all_gather | solution.py:67
  94.2 0.7 broadcast_multiply_fusion
  94.9 0.7 fusion.18
  95.7 0.6 convolution_bitcast_fusion.2
  96.3 1.3 broadcast_in_dim.8
  97.7 7.1 %all-to-all-start.1 = ((f32[32,1,6480]{2,1,0:T(1,128)}), f32[32,1,6480]{2,1,0:T(1,128)}, u32[]{:S(2)}, u32[]{:S(2)}) async-start(f32[32,1,6480]{2,1,0:T(1,128)} %broadcast_in_dim.8), calls=%async_computation.1 | async-start | bytes 1671168 | tf_op jit(solution)/shard_map/all_to_all | solution.py:22
  104.9 0.4 all_to_all.44
  105.3 14.4 %all-to-all-done.1 = f32[32,1,6480]{2,1,0:T(1,128)} async-done(((f32[32,1,6480]{2,1,0:T(1,128)}), f32[32,1,6480]{2,1,0:T(1,128)}, u32[]{:S(2)}, u32[]{:S(2)}) %all-to-all-start.1) | async-done | bytes 829472 | tf_op jit(solution)/shard_map/all_to_all | solution.py:22
  119.7 1.6 %reduce_sum.37 = f32[6480]{0:T(1024)S(1)} reduce(f32[32,1,6480]{2,1,0:T(1,128)} %all-to-all-done.1, f32[]{:T(128)} %constant.44.clone.1), dimensions={0,1}, to_apply=%region_3.4 | reduce | flops 200880 | bytes 855364 | tf_op jit(solution)/shard_map/reduce_sum | solution.py:27
  121.3 0.6 multiply_reduce_fusion
  122.9 0.2 fusion.39
  123.2 0.2 fusion.14
  123.7 0.2 fusion.13
  124.3 0.2 fusion.12
  124.8 0.2 fusion.11
  125.4 0.2 fusion.10
  125.9 0.2 fusion.9
  126.4 0.2 fusion.8
  127.0 0.2 fusion.7
  127.5 0.2 fusion.6
  128.6 0.2 fusion.4
  130.2 0.2 convolution_bitcast_fusion
  130.5 0.6 convolution_convert_fusion
  131.1 0.4 all_to_all.45
  131.5 24.0 %all_to_all.53 = bf16[4,20,8192]{2,1,0:T(8,128)(2,1)S(1)} all-to-all(bf16[4,20,8192]{2,1,0:T(8,128)(2,1)S(1)} %all_to_all.45), channel_id=1, replica_groups=mesh['state'=32,'mem'=4] {'mem'}, dimensions={0} | all-to-all | bytes 2621440 | tf_op jit(solution)/shard_map/all_to_all | solution.py:100
  155.5 1.0 copy.75
  156.6 0.7 pad.6
  157.3 2.0 %copy.81 = bf16[3,8,4,8192]{3,1,2,0:T(8,128)(2,1)} copy(bf16[3,8,4,8192]{3,2,1,0:T(4,128)(2,1)S(1)} %bitcast.113) | data formatting | bytes 3145728
  (56 shorter events, 6.3 us)
Async XLA Ops:
  6.7 17.5 %copy-start = (bf16[20,32768]{1,0:T(8,128)(2,1)S(1)}, bf16[20,32768]{1,0:T(8,128)(2,1)}, u32[]{:S(2)}) copy-start(bf16[20,32768]{1,0:T(8,128)(2,1)} %param.5) | copy-start | bytes 3932164
  24.6 1.1 copy-start.2
  38.2 9.9 %copy-start.1 = (bf16[20,32768]{1,0:T(8,128)(2,1)S(1)}, bf16[20,32768]{1,0:T(8,128)(2,1)}, u32[]{:S(2)}) copy-start(bf16[20,32768]{1,0:T(8,128)(2,1)} %param.5) | copy-start | bytes 3932164
  39.5 18.9 %all-to-all-start = ((f32[32,96,21]{1,2,0:T(8,128)}), f32[32,96,21]{1,2,0:T(8,128)S(1)}, u32[]{:S(2)}, u32[]{:S(2)}) async-start(f32[32,96,21]{1,2,0:T(8,128)} %pad_maximum_fusion), calls=%async_computation | async-start | bytes 786432 | tf_op jit(solution)/shard_map/all_to_all | solution.py:15
  58.3 38.0 %all-to-all-start.2 = ((bf16[20,4,8192]{2,0,1:T(8,128)(2,1)}), bf16[20,4,8192]{2,0,1:T(8,128)(2,1)S(1)}, u32[]{:S(2)}, u32[]{:S(2)}) async-start(bf16[20,4,8192]{2,0,1:T(8,128)(2,1)} %copy.74), calls=%async_computation.2 | async-start | bytes 3145728 | tf_op jit(solution)/shard_map/all_to_all | solution.py:96
  97.7 22.0 %all-to-all-start.1 = ((f32[32,1,6480]{2,1,0:T(1,128)}), f32[32,1,6480]{2,1,0:T(1,128)}, u32[]{:S(2)}, u32[]{:S(2)}) async-start(f32[32,1,6480]{2,1,0:T(1,128)} %broadcast_in_dim.8), calls=%async_computation.1 | async-start | bytes 1671168 | tf_op jit(solution)/shard_map/all_to_all | solution.py:22
where the time goes:
time: 160 us; the launch traced here: 159 us
  local copies, waits for them, and re-layouts  43.1 us (27%)
  blocking collectives  34.9 us (22%)
  other arithmetic  27.3 us (17%)
  starting transfers between devices  20.7 us (13%)
  waiting for transfers between devices  20 us (12%)
  matrix products  11.9 us (7%)
    all_to_all x1, blocking collectives, per_device(): lax.all_to_all(updated, 'mem', split_axis=0, concat_axis=1, tiled=True)  24 us
    scatter-add x1, other arithmetic, per_device(): jax.ops.segment_sum(arrived, arrived_place.astype(jnp.int32), num_segment...  17.5 us
    gather x2, local copies, waits for them, and re-layouts, per_device(): local_place = (slot_ids[order] % share_width).astype(jnp.float32)  17.5 us
    all_to_all x1, waiting for transfers between devices, copy_for_each(): lax.all_to_all(jnp.broadcast_to(x[None], (peers, *x.shape)), axis, 0, 0,...  14.4 us
    all_gather x1, blocking collectives, gather_members(): lax.all_gather(shares.astype(jnp.bfloat16), 'mem', axis=0, tiled=True)  10.9 us
    all_to_all x1, starting transfers between devices, sent_together(): lax.all_to_all(both, axis, split_axis=split_dim, concat_axis=concat_dim,...  8.57 us
    gather x1, local copies, waits for them, and re-layouts, per_device(): sorted_values = values[order]  8.12 us
    all_to_all x1, starting transfers between devices, copy_for_each(): lax.all_to_all(jnp.broadcast_to(x[None], (peers, *x.shape)), axis, 0, 0,...  7.1 us
  transfers between devices with their start and end apart: 3, of which 2 were waited for; matrix products, arithmetic and copies ran while one was open for 15% of the time, Pallas kernels for 0%

commit v1 on v0

--- a/solution.py
+++ b/solution.py
@@ -5,6 +5,28 @@
 from jax.sharding import PartitionSpec as P
 
 ITERS = 14
+
+
+def joined_along(pieces, dim):
+    pieces = jnp.moveaxis(pieces, 0, dim)
+    shape = pieces.shape
+    return pieces.reshape(*shape[:dim], shape[dim] * shape[dim + 1], *shape[dim + 2 :])
+
+
+def collect(shard, axis, dim):
+    size = lax.axis_size(axis)
+    pairs = [(i, (i + 1) % size) for i in range(size)]
+    back = [(b, a) for a, b in pairs]
+    lower, upper = ([], [])
+    for step in range(size - 1):
+        if step % 2 == 0:
+            lower.append(lax.ppermute(lower[-1] if lower else shard, axis, pairs))
+        else:
+            upper.append(lax.ppermute(upper[-1] if upper else shard, axis, back))
+    blocks = jnp.stack([*lower[::-1], shard, *upper])
+    shift = lax.axis_index(axis) - len(lower)
+    blocks = blocks[(jnp.arange(size) - shift) % size]
+    return joined_along(blocks, dim)
 
 
 def sent_together(arrays, axis, split_dim, concat_dim, along):
@@ -64,9 +86,7 @@
 
 
 def gather_members(shares):
-    return lax.all_gather(shares.astype(jnp.bfloat16), "mem", axis=0, tiled=True).astype(
-        jnp.float32
-    )
+    return collect(shares.astype(jnp.bfloat16), "mem", 0).astype(jnp.float32)
 
 
 def per_device(ensemble, weights, seg_obs, observed, inv_var):

time: 160 us -> 175 us (1.094)
  waiting for transfers between devices: 20 us -> 44.9 us
  blocking collectives: 34.9 us -> 23.1 us
    ppermute x0 -> x3, waiting for transfers between devices: none -> 26.2 us  [the longest x2 26.2 us: collect(): lower.append(lax.ppermute(lower[-1] if lower else shard, axis, pairs))]
    all_gather x1 -> x0, blocking collectives: 10.9 us -> none  [gather_members(): lax.all_gather(shares.astype(jnp.bfloat16), 'mem', axis=0, tiled=True)]
    ppermute x0 -> x3, starting transfers between devices: none -> 3.26 us  [the longest x1 1.73 us: collect(): upper.append(lax.ppermute(upper[-1] if upper else shard, axis, back))]
    all_to_all x1, starting transfers between devices: 7.1 us -> 5.05 us  [copy_for_each(): lax.all_to_all(jnp.broadcast_to(x[None], (peers, *x.shape)), axis, 0, 0,...]
    unnamed x11 -> x10, local copies, waits for them, and re-layouts: 5.16 us -> 4.93 us
  transfers between devices with their start and end apart: 3 -> 6, of which waited for: 2 -> 4; matrix products, arithmetic and copies ran while one was open for 15% -> 14% of each run, Pallas kernels for 0% -> 0%
where the time goes in v1:
time: 175 us; the launch traced here: 174 us
  waiting for transfers between devices  44.9 us (26%)
  local copies, waits for them, and re-layouts  44.6 us (25%)
  other arithmetic  26.7 us (15%)
  blocking collectives  23.1 us (13%)
  starting transfers between devices  21.9 us (13%)
  matrix products  11.9 us (7%)
    ppermute x2, waiting for transfers between devices, collect(): lower.append(lax.ppermute(lower[-1] if lower else shard, axis, pairs))  26.2 us
    all_to_all x1, blocking collectives, per_device(): lax.all_to_all(updated, 'mem', split_axis=0, concat_axis=1, tiled=True)  23.1 us
    gather x2, local copies, waits for them, and re-layouts, per_device(): local_place = (slot_ids[order] % share_width).astype(jnp.float32)  17.5 us
    scatter-add x1, other arithmetic, per_device(): jax.ops.segment_sum(arrived, arrived_place.astype(jnp.int32), num_segment...  17.2 us
    all_to_all x1, waiting for transfers between devices, copy_for_each(): lax.all_to_all(jnp.broadcast_to(x[None], (peers, *x.shape)), axis, 0, 0,...  13.2 us
    all_to_all x1, starting transfers between devices, sent_together(): lax.all_to_all(both, axis, split_axis=split_dim, concat_axis=concat_dim,...  8.57 us
    gather x1, local copies, waits for them, and re-layouts, per_device(): sorted_values = values[order]  8.12 us
    sort x1, other arithmetic, per_device(): order = jnp.argsort(owner, stable=True)  5.76 us
  transfers between devices with their start and end apart: 6, of which 4 were waited for; matrix products, arithmetic and copies ran while one was open for 14% of the time, Pallas kernels for 0%

profile of v1, /device:TPU:1, one launch (start us, length us, event | category | flops | bytes accessed | tf_op | source)
XLA Modules:
  0.0 174.4 jit_solution(4677313290568435795)
XLA Ops:
  0.0 0.8 copy.74
  1.0 5.8 %sort.17 = (s32[3072]{0:T(1024)}, s32[3072]{0:T(1024)S(1)}) sort(s32[3072]{0:T(1024)S(1)} %add_select_fusion.1, s32[3072]{0:T(1024)S(1)} %iota.92), dimensions={0}, to_apply=%region_0.1 | sort | flops 36864 | bytes 49152 | tf_op jit(solution)/shard_map/jit(argsort)/sort | solution.py:103
  6.7 17.4 %gather_fusion.1 = s32[3072]{0:T(1024)S(1)} fusion(s32[3072]{0:T(1024)S(1)} %reshape.233, s32[3072]{0:T(1024)S(1)} %fusion.32), kind=kCustom, calls=%fused_computation.1 | custom fusion | bytes 36864 | tf_op jit(solution)/shard_map/gather | solution.py:105
  24.3 0.3 copy.88
  24.7 1.0 copy-done.2
  25.7 2.7 %fusion = f32[256,12,20]{2,1,0:T(8,128)} fusion(bf16[20,256,128]{2,1,0:T(8,128)(2,1)S(1)} %slice.24, bf16[256,12,128]{2,0,1:T(8,128)(2,1)S(1)} %copy-done.2), kind=kOutput, calls=%fused_computation.6 | convolution fusion | flops 15728640 | bytes 2342912 | tf_op jit(solution)/shard_map/ktc,tjc->tjk/dot_general | solution.py:98
  28.4 1.6 reshape.277
  30.0 8.1 %gather_fusion = f32[3072,20]{1,0:T(8,128)S(1)} fusion(f32[3072,20]{1,0:T(8,128)S(1)} %reshape.277, s32[3072]{0:T(1024)S(1)} %fusion.32), kind=kCustom, calls=%fused_computation | custom fusion | bytes 503808 | tf_op jit(solution)/shard_map/gather | solution.py:104
  38.2 0.5 copy.76
  38.7 0.8 pad_maximum_fusion.1
  39.5 8.6 %all-to-all-start = ((f32[32,96,21]{1,2,0:T(8,128)}), f32[32,96,21]{1,2,0:T(8,128)S(1)}, u32[]{:S(2)}, u32[]{:S(2)}) async-start(f32[32,96,21]{1,2,0:T(8,128)} %pad_maximum_fusion.1), calls=%async_computation | async-start | bytes 786432 | tf_op jit(solution)/shard_map/all_to_all | solution.py:37
  48.1 2.1 %all_to_all.41 = bf16[20,4,8192]{2,1,0:T(4,128)(2,1)S(1)} reshape(bf16[20,32768]{1,0:T(8,128)(2,1)S(1)} %copy-done.1) | data formatting | bytes 2621440 | tf_op jit(solution)/shard_map/all_to_all | solution.py:116
  50.2 1.9 %copy.82 = bf16[20,4,8192]{2,0,1:T(8,128)(2,1)} copy(bf16[20,4,8192]{2,1,0:T(4,128)(2,1)S(1)} %all_to_all.41) | data formatting | bytes 2621440 | tf_op jit(solution)/shard_map/all_to_all | solution.py:116
  52.1 0.7 dynamic_slice.6
  52.8 5.6 %all-to-all-done = f32[32,96,21]{1,2,0:T(8,128)S(1)} async-done(((f32[32,96,21]{1,2,0:T(8,128)}), f32[32,96,21]{1,2,0:T(8,128)S(1)}, u32[]{:S(2)}, u32[]{:S(2)}) %all-to-all-start) | async-done | bytes 258080 | tf_op jit(solution)/shard_map/all_to_all | solution.py:37
  58.3 5.0 %all-to-all-start.2 = ((bf16[20,4,8192]{2,0,1:T(8,128)(2,1)}), bf16[20,4,8192]{2,0,1:T(8,128)(2,1)}, u32[]{:S(2)}, u32[]{:S(2)}) async-start(bf16[20,4,8192]{2,0,1:T(8,128)(2,1)} %copy.82), calls=%async_computation.2 | async-start | bytes 3145728 | tf_op jit(solution)/shard_map/all_to_all | solution.py:116
  63.4 0.2 all_to_all.39
  63.7 0.5 copy.79
  64.2 17.2 %scatter_custom_fusion = f32[2048,20]{1,0:T(8,128)S(1)} fusion(s32[3072]{0:T(1024)S(1)} %bitcast.131, f32[3072,20]{1,0:T(8,128)S(1)} %copy.79, f32[]{:T(128)} %constant.62.clone.1), kind=kCustom, calls=%fused_computation.43 | custom fusion | flops 61440 | bytes 163844 | tf_op jit(solution)/shard_map/scatter-add | solution.py:107
  81.5 1.5 collective-permute-start
  83.1 1.7 collective-permute-start.2
  84.8 12.1 %collective-permute-done = bf16[20,2048]{0,1:T(8,128)(2,1)S(1)} collective-permute-done((bf16[20,2048]{0,1:T(8,128)(2,1)S(1)}, bf16[20,2048]{0,1:T(8,128)(2,1)S(1)}, u32[]{:S(2)}, u32[]{:S(2)}) %collective-permute-start) | collective-permute-done | bytes 81952 | tf_op jit(solution)/shard_map/ppermute | solution.py:23
  97.0 14.0 %collective-permute-done.1 = bf16[20,2048]{0,1:T(8,128)(2,1)S(1)} collective-permute-done((bf16[20,2048]{0,1:T(8,128)(2,1)S(1)}, bf16[20,2048]{0,1:T(8,128)(2,1)S(1)}, u32[]{:S(2)}, u32[]{:S(2)}) %collective-permute-start.1) | collective-permute-done | bytes 81952 | tf_op jit(solution)/shard_map/ppermute | solution.py:23
  111.0 0.5 pad_maximum_fusion
  111.5 0.9 copy.80
  112.5 0.6 gather_fusion.2
  113.2 0.7 broadcast_multiply_fusion.1
  114.3 0.7 fusion.42
  115.0 0.6 convolution_bitcast_fusion.2
  115.7 1.3 broadcast_in_dim.8
  117.0 5.1 %all-to-all-start.1 = ((f32[32,1,6480]{2,1,0:T(1,128)}), f32[32,1,6480]{2,1,0:T(1,128)S(1)}, u32[]{:S(2)}, u32[]{:S(2)}) async-start(f32[32,1,6480]{2,1,0:T(1,128)} %broadcast_in_dim.8), calls=%async_computation.1 | async-start | bytes 1671168 | tf_op jit(solution)/shard_map/all_to_all | solution.py:44
  122.2 1.6 all_to_all.44
  123.8 13.2 %all-to-all-done.1 = f32[32,1,6480]{2,1,0:T(1,128)S(1)} async-done(((f32[32,1,6480]{2,1,0:T(1,128)}), f32[32,1,6480]{2,1,0:T(1,128)S(1)}, u32[]{:S(2)}, u32[]{:S(2)}) %all-to-all-start.1) | async-done | bytes 829472 | tf_op jit(solution)/shard_map/all_to_all | solution.py:44
  136.9 0.5 reduce_sum.37
  137.4 0.6 multiply_reduce_fusion
  139.0 0.2 fusion.34
  139.3 0.2 fusion.14
  139.8 0.2 fusion.13
  140.4 0.2 fusion.12
  140.9 0.2 fusion.11
  145.8 0.2 fusion.2
  146.3 0.2 convolution_bitcast_fusion
  146.6 0.6 convolution_convert_fusion
  147.2 0.4 all_to_all.45
  147.6 23.1 %all_to_all.53 = bf16[4,20,8192]{2,1,0:T(8,128)(2,1)S(1)} all-to-all(bf16[4,20,8192]{2,1,0:T(8,128)(2,1)S(1)} %all_to_all.45), channel_id=1, replica_groups=mesh['state'=32,'mem'=4] {'mem'}, dimensions={0} | all-to-all | bytes 2621440 | tf_op jit(solution)/shard_map/all_to_all | solution.py:120
  170.7 1.0 copy.83
  171.7 0.7 pad.11
  172.4 2.0 %copy.89 = bf16[3,8,4,8192]{3,1,2,0:T(8,128)(2,1)} copy(bf16[3,8,4,8192]{3,2,1,0:T(4,128)(2,1)S(1)} %bitcast.121) | data formatting | bytes 3145728
  (68 shorter events, 7.6 us)
Async XLA Ops:
  6.7 17.5 %copy-start = (bf16[20,32768]{1,0:T(8,128)(2,1)S(1)}, bf16[20,32768]{1,0:T(8,128)(2,1)}, u32[]{:S(2)}) copy-start(bf16[20,32768]{1,0:T(8,128)(2,1)} %param.5) | copy-start | bytes 3932164
  24.6 1.1 copy-start.2
  38.2 9.9 %copy-start.1 = (bf16[20,32768]{1,0:T(8,128)(2,1)S(1)}, bf16[20,32768]{1,0:T(8,128)(2,1)}, u32[]{:S(2)}) copy-start(bf16[20,32768]{1,0:T(8,128)(2,1)} %param.5) | copy-start | bytes 3932164
  39.5 18.9 %all-to-all-start = ((f32[32,96,21]{1,2,0:T(8,128)}), f32[32,96,21]{1,2,0:T(8,128)S(1)}, u32[]{:S(2)}, u32[]{:S(2)}) async-start(f32[32,96,21]{1,2,0:T(8,128)} %pad_maximum_fusion.1), calls=%async_computation | async-start | bytes 786432 | tf_op jit(solution)/shard_map/all_to_all | solution.py:37
  58.3 57.4 %all-to-all-start.2 = ((bf16[20,4,8192]{2,0,1:T(8,128)(2,1)}), bf16[20,4,8192]{2,0,1:T(8,128)(2,1)}, u32[]{:S(2)}, u32[]{:S(2)}) async-start(bf16[20,4,8192]{2,0,1:T(8,128)(2,1)} %copy.82), calls=%async_computation.2 | async-start | bytes 3145728 | tf_op jit(solution)/shard_map/all_to_all | solution.py:116
  81.5 15.4 %collective-permute-start = (bf16[20,2048]{0,1:T(8,128)(2,1)S(1)}, bf16[20,2048]{0,1:T(8,128)(2,1)S(1)}, u32[]{:S(2)}, u32[]{:S(2)}) collective-permute-start(bf16[20,2048]{0,1:T(8,128)(2,1)S(1)} %get-tuple-element.8), channel_id=1, source_target_pairs={{0,1},{1,2},{2,3},{3,0},{4,5},{5,6},{6,7},{7,4},{8,9},{9,10},{10,1... | collective-permute-start | bytes 245768 | tf_op jit(solution)/shard_map/ppermute | solution.py:23
  83.1 13.9 %collective-permute-start.2 = (bf16[20,2048]{0,1:T(8,128)(2,1)S(1)}, bf16[20,2048]{0,1:T(8,128)(2,1)S(1)}, u32[]{:S(2)}, u32[]{:S(2)}) collective-permute-start(bf16[20,2048]{0,1:T(8,128)(2,1)S(1)} %get-tuple-element.8), channel_id=1, source_target_pairs={{1,0},{2,1},{3,2},{0,3},{5,4},{6,5},{7,6},{4,7},{9,8},{10,9},{11,1... | collective-permute-start | bytes 245768 | tf_op jit(solution)/shard_map/ppermute | solution.py:25
  96.9 14.1 %collective-permute-start.1 = (bf16[20,2048]{0,1:T(8,128)(2,1)S(1)}, bf16[20,2048]{0,1:T(8,128)(2,1)S(1)}, u32[]{:S(2)}, u32[]{:S(2)}) collective-permute-start(bf16[20,2048]{0,1:T(8,128)(2,1)S(1)} %collective-permute-done), channel_id=1, source_target_pairs={{0,1},{1,2},{2,3},{3,0},{4,5},{5,6},{6,7},{7,4},{8,9},{9,10},{10,1... | collective-permute-start | bytes 245768 | tf_op jit(solution)/shard_map/ppermute | solution.py:23
  117.0 19.9 %all-to-all-start.1 = ((f32[32,1,6480]{2,1,0:T(1,128)}), f32[32,1,6480]{2,1,0:T(1,128)S(1)}, u32[]{:S(2)}, u32[]{:S(2)}) async-start(f32[32,1,6480]{2,1,0:T(1,128)} %broadcast_in_dim.8), calls=%async_computation.1 | async-start | bytes 1671168 | tf_op jit(solution)/shard_map/all_to_all | solution.py:44
